TPU v7x, 512 devices: a whole 4x8x8 slice. The times are simulated.
512 devices in a mesh: replica: 32 (over y, x), owner: 16 (over z, core).
Axes of the slice: x: 4, y: 8, z: 8, core: 2. Of those that a mesh axis runs over, the one named last changes fastest.
Arguments:
- owner_of: int32 [24], replicated, may hold values from 0 to 15, as said below
- grad: bfloat16 [32, 32, 2304, 128], P('replica', 'owner')
- error: bfloat16 [32, 32, 2304, 128], P('replica', 'owner'), may hold values from -4 to 4
- q_prev: float32 [32, 128, 32], P('owner')
- weight: float32 [32, 2304, 128], P('owner', 'replica'), may hold values from -0.125 to 0.125
- momentum: float32 [32, 2304, 128], P('owner', 'replica'), may hold values from -1.2 to 1.2
- vec_grad: bfloat16 [32, 128, 2304], P('replica', 'owner')
- vec_weight: float32 [128, 2304], P('owner', 'replica'), may hold values from 0.5 to 1.5
- vec_mom: float32 [128, 2304], P('owner', 'replica'), may hold values from -1.2 to 1.2
Outputs:
- weight_next: float32 [32, 2304, 128], P('owner', 'replica')
- momentum_next: float32 [32, 2304, 128], P('owner', 'replica')
- error_next: bfloat16 [32, 32, 2304, 128], P('replica', 'owner')
- q_next: float32 [32, 128, 32], P('owner')
- vec_weight_next: float32 [128, 2304], P('owner', 'replica')
- vec_mom_next: float32 [128, 2304], P('owner', 'replica')
Inputs may be any that keep to these rules, and one draw needn't show every extreme that they name: `owner_of`: every owner index appears once or twice; half of them appear twice.
All inputs are finite; a program needn't handle non-finite values.
Results may differ from a plain program's by a relative error of at most 0.001.
Values sent between devices are 32-bit elements; how exact they have to be, the bound alone decides.
A program may use at most 64 MiB of HBM per device.

v0:
```python
import jax
import jax.numpy as jnp
from jax import lax
from jax.sharding import PartitionSpec as P

NS_ITERS = 5
exact_mode = lax.Precision.HIGHEST
clip_limit = 0.1
momentum_decay = 0.9
learn_rate = 0.05


def inverse_root(gram_mat, iterations):
    identity = jnp.eye(gram_mat.shape[-1], dtype=jnp.float32)
    scale_sq = jnp.sqrt(jnp.sum(gram_mat * gram_mat, axis=(1, 2), keepdims=True) + 1e-06)
    current = gram_mat / scale_sq
    inv_root = jnp.broadcast_to(identity, gram_mat.shape)
    for iteration in range(iterations):
        factor_mat = 1.5 * identity - 0.5 * jnp.einsum(
            "sij,sjk->sik", inv_root, current, precision=exact_mode
        )
        current = jnp.einsum("sij,sjk->sik", current, factor_mat, precision=exact_mode)
        inv_root = jnp.einsum("sij,sjk->sik", factor_mat, inv_root, precision=exact_mode)
    return (inv_root, scale_sq)


def on_device(owner_of, grad, error, q_prev, weight, momentum, vec_grad, vec_weight, vec_mom):
    replicas = lax.axis_size("replica")
    owners = lax.axis_size("owner")
    rank_index = lax.axis_index("replica")
    owner_index = lax.axis_index("owner")
    slot_count = grad.shape[1]
    rows_share = weight.shape[1]
    count_own = jnp.sum((owner_of == owner_index).astype(jnp.int32))
    live_slots = jnp.arange(slot_count, dtype=jnp.int32) < count_own
    live_mask = live_slots[:, None, None]
    merged = grad[0].astype(jnp.float32) + error[0].astype(jnp.float32)
    left_terms = jnp.einsum("sdw,swk->sdk", merged, q_prev, precision=exact_mode)
    vec_terms = vec_grad[0].astype(jnp.float32)
    p_sum, vec_sum = lax.psum((left_terms, vec_terms), "replica")
    gram_mat = jnp.einsum("sdi,sdj->sij", p_sum, p_sum, precision=exact_mode)
    inv_root, scale_sq = inverse_root(gram_mat, NS_ITERS)
    p_hat = jnp.einsum("sdi,sij->sdj", p_sum, inv_root, precision=exact_mode) / jnp.sqrt(scale_sq)
    vec_full = vec_sum / replicas
    vec_cols = lax.dynamic_slice_in_dim(vec_full, rank_index * rows_share, rows_share, 1)
    right_terms = jnp.einsum("sdw,sdk->swk", merged, p_hat, precision=exact_mode)
    q_new = lax.psum(right_terms, "replica") / replicas
    approx = jnp.einsum("sdk,swk->sdw", p_hat, q_new, precision=exact_mode)
    error_next = jnp.where(live_mask, (merged - approx).astype(jnp.bfloat16), error[0])
    approx_rows = lax.dynamic_slice_in_dim(approx, rank_index * rows_share, rows_share, 1)
    local_sq = jnp.sum(jnp.where(live_mask, approx * approx, 0.0)) + jnp.sum(vec_full * vec_full)
    total_sq = lax.psum(local_sq, "owner")
    width = merged.shape[1]
    entry_count = float(
        owner_of.shape[0] * width * merged.shape[2] + owners * vec_grad.shape[1] * width
    )
    factor = jnp.minimum(1.0, clip_limit / jnp.sqrt(total_sq / entry_count + 1e-06))
    momentum_next = jnp.where(live_mask, momentum_decay * momentum + factor * approx_rows, momentum)
    weight_next = jnp.where(live_mask, weight - learn_rate * momentum_next, weight)
    q_next = jnp.where(live_mask, q_new, q_prev)
    vec_mom_next = momentum_decay * vec_mom + factor * vec_cols
    vec_weight_next = vec_weight - learn_rate * vec_mom_next
    return (weight_next, momentum_next, error_next[None], q_next, vec_weight_next, vec_mom_next)


def solution(mesh):
    return jax.shard_map(
        on_device,
        mesh=mesh,
        in_specs=(
            P(),
            P("replica", "owner", None, None),
            P("replica", "owner", None, None),
            P("owner", None, None),
            P("owner", "replica", None),
            P("owner", "replica", None),
            P("replica", "owner", None),
            P("owner", "replica"),
            P("owner", "replica"),
        ),
        out_specs=(
            P("owner", "replica", None),
            P("owner", "replica", None),
            P("replica", "owner", None, None),
            P("owner", None, None),
            P("owner", "replica"),
            P("owner", "replica"),
        ),
        check_vma=False,
    )
```

profile of v0, /device:TPU:1, one launch (start us, length us, event | category | flops | bytes accessed | tf_op | source)
XLA Modules:
  0.0 373.0 jit_solution(3170516663309399154)
XLA Ops:
  7.2 0.0 copy-start.9
  7.2 0.0 all-reduce.3.cloned.1.call-start
  7.2 1.4 bitcast_convert_fusion
  8.6 5.1 %fusion.1 = f32[2,2304,32]{1,2,0:T(8,128)} fusion(f32[2,128,32]{1,2,0:T(8,128)} %param.12, bf16[1,2,2304,128]{3,2,1,0:T(8,128)(2,1)} %param.10, bf16[1,2,2304,128]{3,2,1,0:T(8,128)(2,1)} %param.11), kind=kOutput, calls=%fused_computation.5 | convolution fusion | flops 228261888 | bytes 2981888 | tf_op jit(solution)/shard_map/sdw,swk->sdk/dot_general | solution.py:38
  13.7 0.0 all-reduce.3.cloned.1.call-update
  13.8 0.0 copy-done.9
  13.8 0.6 fusion.22
  14.4 0.6 iota_compare_fusion.1
  15.1 159.0 %all-reduce.3.cloned.1.call-done = (f32[2,2304,32]{1,2,0:T(8,128)}, f32[8,2304]{1,0:T(8,128)}) async-done(((f32[2,2304,32]{1,2,0:T(8,128)}, f32[8,2304]{1,0:T(8,128)}), (f32[2,2304,32]{1,2,0:T(8,128)}, f32[8,2304]{1,0:T(8,128)})) %all-reduce.3.cloned.1.call-update) | async-done | bytes 663568 | tf_op jit(solution)/shard_map/psum | solution.py:40
  174.1 2.1 multiply_reduce_fusion.1
  176.2 0.2 fusion.12
  176.5 0.2 fusion.21
  176.7 0.2 fusion.16
  176.9 0.2 fusion.11
  177.1 0.2 fusion.26
  177.2 0.2 fusion.25
  177.4 0.2 fusion.10
  177.6 0.2 fusion.28
  177.8 0.2 fusion.27
  177.9 0.2 fusion.9
  178.1 0.2 fusion.29
  178.3 0.2 fusion.30
  178.4 0.0 copy-done.4
  178.4 0.6 broadcast_multiply_fusion
  179.1 0.2 fusion.8
  179.2 0.2 fusion.31
  179.5 0.0 copy-done.2
  179.5 0.6 convolution_divide_fusion
  180.1 0.0 copy-done
  180.1 0.0 copy-done.1
  180.1 0.0 copy-start.3
  180.1 1.6 fusion
  181.8 113.6 %psum.29 = f32[2,128,32]{1,2,0:T(8,128)S(1)} all-reduce(f32[2,128,32]{1,2,0:T(8,128)S(1)} %fusion), channel_id=1, replica_groups=mesh['replica'=32,'owner'=16] {'replica'}, use_global_device_ids=true, to_apply=%region_3.0 | all-reduce | flops 8192 | bytes 65536 | tf_op jit(solution)/shard_map/psum | solution.py:47
  295.4 5.9 %select_reduce_fusion = (f32[]{:T(128)}, f32[2,2304,128]{2,1,0:T(8,128)}) fusion(pred[2]{0:T(512)(128)(4,1)S(1)} %iota_compare_fusion.1, f32[2,2304,32]{1,2,0:T(8,128)S(1)} %convolution_divide_fusion, f32[2,128,32]{1,2,0:T(8,128)S(1)} %psum.29), kind=kOutput, calls=%fused_computation.3 | convolution fusion | flops 228270080 | bytes 2981894 | tf_op jit(solution)/shard_map/sdk,swk->sdw/dot_general | solution.py:48
  302.6 0.0 copy-done.3
  302.6 0.7 multiply_select_fusion
  303.3 56.5 %psum.31 = f32[]{:T(128)} all-reduce(f32[]{:T(128)S(6)} %add.40), channel_id=1, replica_groups=mesh['replica'=32,'owner'=16] {'owner'}, use_global_device_ids=true, to_apply=%region_7.8 | all-reduce | flops 1 | bytes 8 | tf_op jit(solution)/shard_map/psum | solution.py:52
  360.5 0.0 copy-start.5
  360.5 0.0 copy-start.6
  360.6 0.0 copy-start.7
  360.6 0.0 copy-start.8
  360.6 3.2 fusion.3
  363.8 0.0 copy-done.5
  363.8 0.0 copy-done.6
  363.8 1.6 subtract_select_fusion
  365.5 0.0 copy-done.7
  365.5 0.0 copy-done.8
  365.5 0.7 multiply_subtract_fusion
  (7 shorter events, 0.0 us)
Async XLA Ops:
  7.2 6.6 %copy-start.9 = (s32[24]{0:T(128)S(1)}, s32[24]{0:T(128)}, u32[]{:S(2)}) copy-start(s32[24]{0:T(128)} %param.9) | copy-start | bytes 292
  7.2 166.9 %all-reduce.3.cloned.1.call-start = ((), (), s32[]{:S(2)}) async-start(), calls=%async_computation | async-start | bytes 1327104 | tf_op jit(solution)/shard_map/psum | solution.py:40
  174.1 4.4 %copy-start.4 = (f32[8,2304]{1,0:T(8,128)S(1)}, f32[8,2304]{1,0:T(8,128)}, u32[]{:S(2)}) copy-start(f32[8,2304]{1,0:T(8,128)} %get-tuple-element.7) | copy-start | bytes 221188
  174.1 5.4 %copy-start.2 = (f32[2,2304,32]{1,2,0:T(8,128)S(1)}, f32[2,2304,32]{1,2,0:T(8,128)}, u32[]{:S(2)}) copy-start(f32[2,2304,32]{1,2,0:T(8,128)} %get-tuple-element.6) | copy-start | bytes 1769476
  174.1 6.0 %copy-start = (bf16[1,2,2304,128]{3,2,1,0:T(8,128)(2,1)S(1)}, bf16[1,2,2304,128]{3,2,1,0:T(8,128)(2,1)}, u32[]{:S(2)}) copy-start(bf16[1,2,2304,128]{3,2,1,0:T(8,128)(2,1)} %param.10) | copy-start | bytes 3538948
  174.1 6.0 %copy-start.1 = (bf16[1,2,2304,128]{3,2,1,0:T(8,128)(2,1)S(1)}, bf16[1,2,2304,128]{3,2,1,0:T(8,128)(2,1)}, u32[]{:S(2)}) copy-start(bf16[1,2,2304,128]{3,2,1,0:T(8,128)(2,1)} %param.11) | copy-start | bytes 3538948
  180.1 122.5 %copy-start.3 = (f32[2,128,32]{1,2,0:T(8,128)S(1)}, f32[2,128,32]{1,2,0:T(8,128)}, u32[]{:S(2)}) copy-start(f32[2,128,32]{1,2,0:T(8,128)} %param.12) | copy-start | bytes 98308
  360.5 3.3 copy-start.5
  360.5 3.3 copy-start.6
  360.6 4.9 %copy-start.7 = (f32[8,72]{1,0:T(8,128)S(1)}, f32[8,72]{1,0:T(8,128)}, u32[]{:S(2)}) copy-start(f32[8,72]{1,0:T(8,128)} %param.16) | copy-start | bytes 6916
  360.6 4.9 %copy-start.8 = (f32[8,72]{1,0:T(8,128)S(1)}, f32[8,72]{1,0:T(8,128)}, u32[]{:S(2)}) copy-start(f32[8,72]{1,0:T(8,128)} %param.17) | copy-start | bytes 6916
Sparse Core Ops, SparseCore 0:
  13.9 160.1 all-reduce.2
where the time goes:
time: 373 us
  blocking collectives  170 us (46%)
  waiting for transfers between devices  159 us (43%)
  matrix products  17.9 us (5%)
  between operations  16.3 us (4%)
  other arithmetic  9.55 us (3%)
    psum x1, waiting for transfers between devices, on_device(): p_sum, vec_sum = lax.psum((left_terms, vec_terms), 'replica')  159 us
    psum x1, blocking collectives, on_device(): q_new = lax.psum(right_terms, 'replica') / replicas  114 us
    psum x1, blocking collectives, on_device(): total_sq = lax.psum(local_sq, 'owner')  56.5 us
  transfers between devices with their start and end apart: 1, of which 1 were waited for; matrix products, arithmetic and copies ran while one was open for 0% of the time, Pallas kernels for 0%

commit v1 on v0

--- a/solution.py
+++ b/solution.py
@@ -25,6 +25,10 @@
 
 
 def on_device(owner_of, grad, error, q_prev, weight, momentum, vec_grad, vec_weight, vec_mom):
+
+    def see_the_positions(local_block, row_axis="replica"):
+        return jnp.sum(lax.all_gather(local_block, axis_name=row_axis), 0)
+
     replicas = lax.axis_size("replica")
     owners = lax.axis_size("owner")
     rank_index = lax.axis_index("replica")
@@ -44,7 +48,7 @@
     vec_full = vec_sum / replicas
     vec_cols = lax.dynamic_slice_in_dim(vec_full, rank_index * rows_share, rows_share, 1)
     right_terms = jnp.einsum("sdw,sdk->swk", merged, p_hat, precision=exact_mode)
-    q_new = lax.psum(right_terms, "replica") / replicas
+    q_new = see_the_positions(right_terms) / replicas
     approx = jnp.einsum("sdk,swk->sdw", p_hat, q_new, precision=exact_mode)
     error_next = jnp.where(live_mask, (merged - approx).astype(jnp.bfloat16), error[0])
     approx_rows = lax.dynamic_slice_in_dim(approx, rank_index * rows_share, rows_share, 1)

time: 373 us -> 314 us (0.84)
  blocking collectives: 170 us -> 29.5 us
  waiting for transfers between devices: 159 us -> 238 us
    psum x1 -> x0, blocking collectives: 114 us -> none  [on_device(): q_new = lax.psum(right_terms, 'replica') / replicas]
    all_gather x0 -> x1, waiting for transfers between devices: none -> 77.5 us  [see_the_positions(): return jnp.sum(lax.all_gather(local_block, axis_name=row_axis), 0)]
    psum x1, blocking collectives: 56.5 us -> 29.5 us  [on_device(): total_sq = lax.psum(local_sq, 'owner')]
  transfers between devices with their start and end apart: 1 -> 2, of which waited for: 1 -> 2; matrix products, arithmetic and copies ran while one was open for 0% -> 1% of each run, Pallas kernels for 0% -> 0%
where the time goes in v1:
time: 314 us
  waiting for transfers between devices  238 us (76%)
  blocking collectives  29.5 us (9%)
  matrix products  19.5 us (6%)
  between operations  16.3 us (5%)
  other arithmetic  10.8 us (3%)
    psum x1, waiting for transfers between devices, on_device(): p_sum, vec_sum = lax.psum((left_terms, vec_terms), 'replica')  160 us
    all_gather x1, waiting for transfers between devices, see_the_positions(): return jnp.sum(lax.all_gather(local_block, axis_name=row_axis), 0)  77.5 us
    psum x1, blocking collectives, on_device(): total_sq = lax.psum(local_sq, 'owner')  29.5 us
  transfers between devices with their start and end apart: 2, of which 2 were waited for; matrix products, arithmetic and copies ran while one was open for 1% of the time, Pallas kernels for 0%

profile of v1, /device:TPU:1, one launch (start us, length us, event | category | flops | bytes accessed | tf_op | source)
XLA Modules:
  0.0 314.0 jit_solution(10600976711058946783)
XLA Ops:
  7.2 0.0 all-reduce.3.cloned.1.call-start
  7.2 1.4 bitcast_convert_fusion
  8.6 5.1 %fusion.1 = f32[2,2304,32]{1,2,0:T(8,128)} fusion(f32[2,128,32]{1,2,0:T(8,128)} %param.12, bf16[1,2,2304,128]{3,2,1,0:T(8,128)(2,1)} %param.10, bf16[1,2,2304,128]{3,2,1,0:T(8,128)(2,1)} %param.11), kind=kOutput, calls=%fused_computation.5 | convolution fusion | flops 228261888 | bytes 2981888 | tf_op jit(solution)/shard_map/sdw,swk->sdk/dot_general | solution.py:42
  13.7 0.0 all-reduce.3.cloned.1.call-update
  13.7 0.0 all-gather.3.cloned.1.call-start
  13.8 0.0 copy-start
  13.8 0.0 copy-start.1
  13.8 160.2 %all-reduce.3.cloned.1.call-done = (f32[2,2304,32]{1,2,0:T(8,128)}, f32[8,2304]{1,0:T(8,128)}) async-done(((f32[2,2304,32]{1,2,0:T(8,128)}, f32[8,2304]{1,0:T(8,128)}), (f32[2,2304,32]{1,2,0:T(8,128)}, f32[8,2304]{1,0:T(8,128)})) %all-reduce.3.cloned.1.call-update) | async-done | bytes 663568 | tf_op jit(solution)/shard_map/psum | solution.py:44
  174.1 2.0 multiply_reduce_fusion.1
  176.1 0.2 fusion.12
  176.3 0.2 fusion.21
  176.6 0.2 fusion.16
  176.7 0.2 fusion.11
  176.9 0.2 fusion.26
  177.1 0.2 fusion.25
  177.2 0.2 fusion.10
  177.4 0.2 fusion.28
  177.6 0.2 fusion.27
  177.7 0.2 fusion.9
  177.9 0.2 fusion.29
  178.1 0.2 fusion.30
  178.3 0.2 fusion.8
  178.4 0.2 fusion.31
  178.7 0.0 copy-start.8
  178.7 0.0 copy-start.3
  178.7 1.7 convolution_divide_fusion
  180.4 0.0 copy-done
  180.4 0.0 copy-done.1
  180.4 2.3 fusion
  182.7 0.0 all-gather.3.cloned.1.call-update
  182.7 0.0 copy-done.8
  182.7 0.6 fusion.22
  183.4 0.6 iota_compare_fusion.1
  184.0 0.0 copy-done.3
  184.0 0.6 broadcast_multiply_fusion
  184.7 77.5 %all-gather.3.cloned.1.call-done = f32[64,128,32]{1,2,0:T(8,128)} async-done(((f32[2,128,32]{1,2,0:T(8,128)}), f32[64,128,32]{1,2,0:T(8,128)}) %all-gather.3.cloned.1.call-update) | async-done | bytes 1048592 | tf_op jit(solution)/shard_map/all_gather | solution.py:30
  262.2 1.3 reduce_sum.47
  263.5 5.9 %select_reduce_fusion = (f32[]{:T(128)}, f32[2,2304,128]{2,1,0:T(8,128)}) fusion(pred[2]{0:T(512)(128)(4,1)S(1)} %iota_compare_fusion.1, f32[2,2304,32]{1,2,0:T(8,128)S(1)} %convolution_divide_fusion, f32[2,128,32]{1,2,0:T(8,128)S(1)} %reduce_sum.47), kind=kOutput, calls=%fused_computation.3 | convolution fusion | flops 228270080 | bytes 2981894 | tf_op jit(solution)/shard_map/sdk,swk->sdw/dot_general | solution.py:52
  270.7 0.0 copy-done.2
  270.7 0.7 multiply_select_fusion
  271.4 29.5 %psum.23 = f32[]{:T(128)} all-reduce(f32[]{:T(128)S(6)} %add.38), channel_id=1, replica_groups=mesh['replica'=32,'owner'=16] {'owner'}, use_global_device_ids=true, to_apply=%region_7.8 | all-reduce | flops 1 | bytes 8 | tf_op jit(solution)/shard_map/psum | solution.py:56
  301.6 0.0 copy-start.4
  301.6 0.0 copy-start.5
  301.6 0.0 copy-start.6
  301.6 0.0 copy-start.7
  301.6 3.2 %fusion.3 = bf16[1,2,2304,128]{3,2,1,0:T(8,128)(2,1)} fusion(f32[2,2304,128]{2,1,0:T(8,128)} %get-tuple-element.19, bf16[1,2,2304,128]{3,2,1,0:T(8,128)(2,1)S(1)} %copy-done, bf16[1,2,2304,128]{3,2,1,0:T(8,128)(2,1)S(1)} %copy-done.1, pred[2]{0:T(512)(128)(4,1)S(1)} %iota_compare_fusion.1), kind=kLoop, calls=%fused_computation.7 | loop fusion | flops 3538944 | bytes 5898242 | tf_op jit(solution)/shard_map/broadcast_in_dim | solution.py:67
  304.9 1.6 subtract_select_fusion
  306.5 0.7 multiply_subtract_fusion
  (8 shorter events, 0.0 us)
Async XLA Ops:
  7.2 166.9 %all-reduce.3.cloned.1.call-start = ((), (), s32[]{:S(2)}) async-start(), calls=%async_computation.1 | async-start | bytes 1327104 | tf_op jit(solution)/shard_map/psum | solution.py:44
  13.7 248.4 %all-gather.3.cloned.1.call-start = ((), (), s32[]{:S(2)}) async-start(), calls=%async_computation | async-start | bytes 1081344 | tf_op jit(solution)/shard_map/all_gather | solution.py:30
  13.8 166.6 %copy-start = (bf16[1,2,2304,128]{3,2,1,0:T(8,128)(2,1)S(1)}, bf16[1,2,2304,128]{3,2,1,0:T(8,128)(2,1)}, u32[]{:S(2)}) copy-start(bf16[1,2,2304,128]{3,2,1,0:T(8,128)(2,1)} %param.10) | copy-start | bytes 3538948
  13.8 166.6 %copy-start.1 = (bf16[1,2,2304,128]{3,2,1,0:T(8,128)(2,1)S(1)}, bf16[1,2,2304,128]{3,2,1,0:T(8,128)(2,1)}, u32[]{:S(2)}) copy-start(bf16[1,2,2304,128]{3,2,1,0:T(8,128)(2,1)} %param.11) | copy-start | bytes 3538948
  178.7 4.1 %copy-start.8 = (s32[24]{0:T(128)S(1)}, s32[24]{0:T(128)}, u32[]{:S(2)}) copy-start(s32[24]{0:T(128)} %param.9) | copy-start | bytes 292
  178.7 5.4 %copy-start.3 = (f32[8,2304]{1,0:T(8,128)S(1)}, f32[8,2304]{1,0:T(8,128)}, u32[]{:S(2)}) copy-start(f32[8,2304]{1,0:T(8,128)} %get-tuple-element.7) | copy-start | bytes 221188
  182.7 88.0 %copy-start.2 = (f32[2,128,32]{1,2,0:T(8,128)S(1)}, f32[2,128,32]{1,2,0:T(8,128)}, u32[]{:S(2)}) copy-start(f32[2,128,32]{1,2,0:T(8,128)} %param.12) | copy-start | bytes 98308
  301.6 3.3 %copy-start.4 = (f32[2,72,128]{2,1,0:T(8,128)S(1)}, f32[2,72,128]{2,1,0:T(8,128)}, u32[]{:S(2)}) copy-start(f32[2,72,128]{2,1,0:T(8,128)} %param.13) | copy-start | bytes 221188
  301.6 3.3 %copy-start.5 = (f32[2,72,128]{2,1,0:T(8,128)S(1)}, f32[2,72,128]{2,1,0:T(8,128)}, u32[]{:S(2)}) copy-start(f32[2,72,128]{2,1,0:T(8,128)} %param.14) | copy-start | bytes 221188
  301.6 4.9 %copy-start.6 = (f32[8,72]{1,0:T(8,128)S(1)}, f32[8,72]{1,0:T(8,128)}, u32[]{:S(2)}) copy-start(f32[8,72]{1,0:T(8,128)} %param.16) | copy-start | bytes 6916
  301.6 4.9 %copy-start.7 = (f32[8,72]{1,0:T(8,128)S(1)}, f32[8,72]{1,0:T(8,128)}, u32[]{:S(2)}) copy-start(f32[8,72]{1,0:T(8,128)} %param.17) | copy-start | bytes 6916
Sparse Core Ops, SparseCore 0:
  13.9 160.1 all-reduce.2
  182.9 79.2 all-gather.2
